TPU v7x, 32 devices: a whole 2x2x4 slice. The times are simulated.
32 devices in a mesh: island: 4 (over y, core), section: 4 (over z), tensor: 2 (over x).
Axes of the slice: x: 2, y: 2, z: 4, core: 2. Of those that a mesh axis runs over, the one named last changes fastest.
Arguments:
- hidden: bfloat16 [4, 4, 256, 8192], P('island', 'section', 'tensor'), may hold values from -6 to 6
- norm_gain: bfloat16 [4, 8192], P('section'), may hold values from 0.099609375 to 1.8984375
- grad_above: bfloat16 [4, 256, 8192], P('island', 'tensor'), may hold values from -6 to 6
- key_cot: bfloat16 [4, 4, 256, 1024], P('island', 'section', None, 'tensor'), may hold values from -6 to 6
- value_cot: bfloat16 [4, 4, 256, 1024], P('island', 'section', None, 'tensor'), may hold values from -6 to 6
- local_key: bfloat16 [4, 4, 8192, 1024], P('island', 'section', None, 'tensor'), may hold values from -6 to 6
- local_value: bfloat16 [4, 4, 8192, 1024], P('island', 'section', None, 'tensor'), may hold values from -6 to 6
- anchor_key: float32 [4, 8192, 1024], P('section', 'island', 'tensor'), may hold values from -6 to 6
- anchor_value: float32 [4, 8192, 1024], P('section', 'island', 'tensor'), may hold values from -6 to 6
- momentum_key: float32 [4, 8192, 1024], P('section', 'island', 'tensor'), may hold values from -4 to 4
- momentum_value: float32 [4, 8192, 1024], P('section', 'island', 'tensor'), may hold values from -4 to 4
Outputs:
- anchor_key_new: float32 [4, 8192, 1024], P('section', 'island', 'tensor')
- anchor_value_new: float32 [4, 8192, 1024], P('section', 'island', 'tensor')
- momentum_key_new: float32 [4, 8192, 1024], P('section', 'island', 'tensor')
- momentum_value_new: float32 [4, 8192, 1024], P('section', 'island', 'tensor')
- input_grad: bfloat16 [4, 4, 256, 8192], P('island', 'section', 'tensor')
All inputs are finite; a program needn't handle non-finite values.
Results may differ from a plain program's by a relative error of at most 0.024.
Values may be sent and summed in bfloat16 or wider, within the bound.
No kernel may reach another device: no remote copies, remote signals or barrier semaphores. Data moves between devices by JAX's collectives and lax.ppermute only.
A program may use at most 128 MiB of HBM per device.

v0:
```python
import jax
import jax.numpy as jnp
from jax import lax
from jax.sharding import PartitionSpec as P

epsilon = 1e-05
inner_rate = 0.5
outer_rate = 0.7
outer_beta = 0.9


def from_behind(block, axis, distance):
    devices = range(lax.axis_size(axis))
    route = [(i - distance, i) for i in devices if i - distance in devices]
    return lax.ppermute(block, axis, route)


def contract_rows(left, right):
    return lax.dot_general(
        left, right, (((0,), (0,)), ((), ())), preferred_element_type=jnp.float32
    )


def contract_cols(left, right):
    return lax.dot_general(
        left, right, (((1,), (1,)), ((), ())), preferred_element_type=jnp.float32
    )


def outer_update(anchor, momentum, mean_delta):
    momentum_new = outer_beta * momentum + mean_delta
    return (anchor - outer_rate * (mean_delta + outer_beta * momentum_new), momentum_new)


def local(
    hidden,
    norm_gain,
    grad_above,
    key_cot,
    value_cot,
    local_key,
    local_value,
    anchor_key,
    anchor_value,
    momentum_key,
    momentum_value,
):
    resid = hidden[0, 0].astype(jnp.float32)
    gains = norm_gain[0].astype(jnp.float32)
    features = resid.shape[1]
    factor = float(features) ** (-0.5)
    inverse_rms = lax.rsqrt(jnp.mean(resid * resid, axis=-1, keepdims=True) + epsilon)
    normed = (resid * inverse_rms * gains).astype(jnp.bfloat16)
    key_rows = key_cot[0, 0]
    value_rows = value_cot[0, 0]
    weight_key = local_key[0, 0]
    weight_value = local_value[0, 0]
    piece = lax.all_gather(normed, "tensor", axis=0, tiled=True)
    key_piece = key_rows
    value_piece = value_rows
    grad_key = contract_rows(piece, key_piece)
    grad_value = contract_rows(piece, value_piece)
    new_key = weight_key.astype(jnp.float32) - inner_rate * (grad_key * factor)
    new_value = weight_value.astype(jnp.float32) - inner_rate * (grad_value * factor)
    key_piece = key_rows
    value_piece = value_rows
    upstream = lax.psum_scatter(
        (
            (contract_cols(key_piece, weight_key) + contract_cols(value_piece, weight_value))
            * factor
        ).astype(jnp.bfloat16),
        "tensor",
        scatter_dimension=0,
        tiled=True,
    ).astype(jnp.float32)
    scaled = gains * upstream
    branch = inverse_rms * scaled - resid * inverse_rms**3 * jnp.mean(
        resid * scaled, axis=-1, keepdims=True
    )
    is_top = (lax.axis_index("section") == lax.axis_size("section") - 1).astype(jnp.float32)
    own_term = branch + is_top * grad_above[0].astype(jnp.float32)
    running = own_term
    for turn in range(lax.axis_size("section") - 1):
        running = own_term + from_behind(running.astype(jnp.bfloat16), "section", -1).astype(
            running.dtype
        )
    input_grad = running.astype(jnp.bfloat16)[None, None]
    islands = lax.axis_size("island")
    summed_key, summed_value = (
        lax.psum_scatter(
            new_key.astype(jnp.bfloat16), "island", scatter_dimension=0, tiled=True
        ).astype(jnp.float32),
        lax.psum_scatter(
            new_value.astype(jnp.bfloat16), "island", scatter_dimension=0, tiled=True
        ).astype(jnp.float32),
    )
    mean_key = anchor_key[0] - summed_key / islands
    mean_value = anchor_value[0] - summed_value / islands
    anchor_key_new, momentum_key_new = outer_update(anchor_key[0], momentum_key[0], mean_key)
    anchor_value_new, momentum_value_new = outer_update(
        anchor_value[0], momentum_value[0], mean_value
    )
    return (
        anchor_key_new[None],
        anchor_value_new[None],
        momentum_key_new[None],
        momentum_value_new[None],
        input_grad,
    )


def solution(mesh):
    placed = (
        P("island", "section", "tensor", None),
        P("section", None),
        P("island", "tensor", None),
        P("island", "section", None, "tensor"),
        P("island", "section", None, "tensor"),
        P("island", "section", None, "tensor"),
        P("island", "section", None, "tensor"),
        P("section", "island", "tensor"),
        P("section", "island", "tensor"),
        P("section", "island", "tensor"),
        P("section", "island", "tensor"),
    )
    return jax.shard_map(
        local,
        mesh=mesh,
        in_specs=placed,
        out_specs=(
            P("section", "island", "tensor"),
            P("section", "island", "tensor"),
            P("section", "island", "tensor"),
            P("section", "island", "tensor"),
            P("island", "section", "tensor", None),
        ),
        check_vma=False,
    )
```

profile of v0, /device:TPU:0, one launch (start us, length us, event | category | flops | bytes accessed | tf_op | source)
XLA Modules:
  0.0 336.5 jit_solution(11189967100800048256)
XLA Ops:
  7.2 0.0 copy-start
  7.2 0.0 reduce-scatter.8.cloned.1.call-start
  7.2 0.9 copy-done
  8.1 5.8 %fusion.3 = f32[256,8192]{1,0:T(8,128)S(1)} fusion(bf16[1,1,8192,512]{3,2,1,0:T(8,128)(2,1)} %param.16, bf16[1,1,256,512]{3,2,1,0:T(8,128)(2,1)S(1)} %copy-done), kind=kOutput, calls=%fused_computation.6 | convolution fusion | flops 2147483648 | bytes 17039360 | tf_op jit(solution)/shard_map/dot_general | solution.py:25
  13.9 7.9 %fusion.1 = bf16[256,8192]{1,0:T(8,128)(2,1)} fusion(f32[256,8192]{1,0:T(8,128)S(1)} %fusion.3, bf16[1,1,8192,512]{3,2,1,0:T(8,128)(2,1)} %param.17, bf16[1,1,256,512]{3,2,1,0:T(8,128)(2,1)S(1)} %copy-done.7), kind=kOutput, calls=%fused_computation.4 | convolution fusion | flops 2153775104 | bytes 21233664 | tf_op jit(solution)/shard_map/dot_general | solution.py:25
  21.8 0.0 reduce-scatter.8.cloned.1.call-update
  21.8 0.0 all-gather.2.cloned.1.call-start
  21.9 0.7 copy-done.8
  22.6 56.5 %reduce-scatter.8.cloned.1.call-done = bf16[128,8192]{1,0:T(8,128)(2,1)} async-done(((bf16[256,8192]{1,0:T(8,128)(2,1)}), bf16[128,8192]{1,0:T(8,128)(2,1)}) %reduce-scatter.8.cloned.1.call-update) | async-done | bytes 2097168 | tf_op jit(solution)/shard_map/reduce_scatter | solution.py:67
  79.1 2.8 fusion.11
  81.9 0.0 copy-done.5
  81.9 4.3 %fusion.21 = (bf16[128,8192]{1,0:T(8,128)(2,1)}, f32[128,8192]{1,0:T(8,128)}, bf16[128,8192]{1,0:T(8,128)(2,1)}) fusion(bf16[1,128,8192]{2,1,0:T(8,128)(2,1)S(1)} %copy-done.5, f32[]{:T(128)S(6)} %convert_element_type.74, f32[128]{0:T(128)S(1)} %get-tuple-element.16, f32[128]{0:T(128)S(1)} %get-tuple-element.14, bf16[1,1,128,8192]{3,2,1,0:T(8,128)(2,1)S(1)} %copy-done.3, ...), kind=kLoop, calls=%fused_computation.41 | loop fusion | flops 14680064 | bytes 14714372 | tf_op jit(solution)/shard_map/convert_element_type | solution.py:84
  86.3 0.0 all-gather.2.cloned.1.call-update
  86.3 0.0 reduce-scatter.4.cloned.1.call-start
  86.3 56.8 %all-gather.2.cloned.1.call-done = bf16[256,8192]{1,0:T(8,128)(2,1)} async-done(((bf16[128,8192]{1,0:T(8,128)(2,1)}), bf16[256,8192]{1,0:T(8,128)(2,1)}) %all-gather.2.cloned.1.call-update) | async-done | bytes 4194320 | tf_op jit(solution)/shard_map/all_gather | solution.py:58
  143.2 8.2 %subtract_convert_fusion.1 = bf16[8192,512]{1,0:T(8,128)(2,1)} fusion(bf16[256,8192]{1,0:T(8,128)(2,1)} %all-gather.2.cloned.1.call-done, bf16[1,1,8192,512]{3,2,1,0:T(8,128)(2,1)} %param.16, bf16[1,1,256,512]{3,2,1,0:T(8,128)(2,1)S(1)} %copy-done), kind=kOutput, calls=%fused_computation.1 | convolution fusion | flops 2164260864 | bytes 21233664 | tf_op jit(solution)/shard_map/dot_general | solution.py:19
  151.3 0.0 reduce-scatter.4.cloned.1.call-update
  151.4 0.0 reduce-scatter.6.cloned.1.call-start
  151.4 8.7 %subtract_convert_fusion = bf16[8192,512]{1,0:T(8,128)(2,1)} fusion(bf16[256,8192]{1,0:T(8,128)(2,1)} %all-gather.2.cloned.1.call-done, bf16[1,1,8192,512]{3,2,1,0:T(8,128)(2,1)} %param.17, bf16[1,1,256,512]{3,2,1,0:T(8,128)(2,1)S(1)} %copy-done.7), kind=kOutput, calls=%fused_computation | convolution fusion | flops 2164260864 | bytes 21233664 | tf_op jit(solution)/shard_map/dot_general | solution.py:19
  160.1 0.0 reduce-scatter.6.cloned.1.call-update
  160.1 2.1 copy-done.6
  162.3 1.3 collective-permute-start
  163.6 47.8 %collective-permute-done = bf16[128,8192]{1,0:T(8,128)(2,1)S(1)} collective-permute-done((bf16[128,8192]{1,0:T(8,128)(2,1)S(1)}, bf16[128,8192]{1,0:T(8,128)(2,1)S(1)}, u32[]{:S(2)}, u32[]{:S(2)}) %collective-permute-start) | collective-permute-done | bytes 2097184 | tf_op jit(solution)/shard_map/ppermute | solution.py:15
  211.3 2.9 add_convert_fusion.2
  214.2 1.3 collective-permute-start.1
  215.5 47.1 %collective-permute-done.1 = bf16[128,8192]{1,0:T(8,128)(2,1)S(1)} collective-permute-done((bf16[128,8192]{1,0:T(8,128)(2,1)S(1)}, bf16[128,8192]{1,0:T(8,128)(2,1)S(1)}, u32[]{:S(2)}, u32[]{:S(2)}) %collective-permute-start.1) | collective-permute-done | bytes 2097184 | tf_op jit(solution)/shard_map/ppermute | solution.py:15
  262.6 0.4 add_convert_fusion.1
  263.0 1.5 collective-permute-start.2
  264.5 46.1 %collective-permute-done.2 = bf16[128,8192]{1,0:T(8,128)(2,1)S(1)} collective-permute-done((bf16[128,8192]{1,0:T(8,128)(2,1)S(1)}, bf16[128,8192]{1,0:T(8,128)(2,1)S(1)}, u32[]{:S(2)}, u32[]{:S(2)}) %collective-permute-start.2) | collective-permute-done | bytes 2097184 | tf_op jit(solution)/shard_map/ppermute | solution.py:15
  310.6 1.8 fusion.16
  312.4 8.7 %fusion.14 = (f32[1,2048,512]{2,1,0:T(8,128)}, f32[1,2048,512]{2,1,0:T(8,128)}) fusion(bf16[2048,512]{1,0:T(8,128)(2,1)} %reduce-scatter.4.cloned.1.call-done, f32[1,2048,512]{2,1,0:T(8,128)} %param.18, f32[1,2048,512]{2,1,0:T(8,128)} %param.20), kind=kLoop, calls=%fused_computation.31 | loop fusion | flops 9437184 | bytes 18874368 | tf_op jit(solution)/shard_map/broadcast_in_dim | solution.py:106
  321.2 8.8 %fusion.15 = (f32[1,2048,512]{2,1,0:T(8,128)}, f32[1,2048,512]{2,1,0:T(8,128)}) fusion(bf16[2048,512]{1,0:T(8,128)(2,1)} %reduce-scatter.6.cloned.1.call-done, f32[1,2048,512]{2,1,0:T(8,128)} %param.19, f32[1,2048,512]{2,1,0:T(8,128)} %param.21), kind=kLoop, calls=%fused_computation.32 | loop fusion | flops 9437184 | bytes 18874368 | tf_op jit(solution)/shard_map/broadcast_in_dim | solution.py:107
  (17 shorter events, 0.1 us)
Async XLA Ops:
  7.2 1.0 copy-start
  7.2 6.7 %copy-start.7 = (bf16[1,1,256,512]{3,2,1,0:T(8,128)(2,1)S(1)}, bf16[1,1,256,512]{3,2,1,0:T(8,128)(2,1)}, u32[]{:S(2)}) copy-start(bf16[1,1,256,512]{3,2,1,0:T(8,128)(2,1)} %param.15) | copy-start | bytes 786436
  7.2 71.9 %reduce-scatter.8.cloned.1.call-start = ((), (), s32[]{:S(2)}) async-start(), calls=%async_computation.6 | async-start | bytes 6291456 | tf_op jit(solution)/shard_map/reduce_scatter | solution.py:67
  21.8 0.8 copy-start.8
  21.8 57.3 %copy-start.3 = (bf16[1,1,128,8192]{3,2,1,0:T(8,128)(2,1)S(1)}, bf16[1,1,128,8192]{3,2,1,0:T(8,128)(2,1)}, u32[]{:S(2)}) copy-start(bf16[1,1,128,8192]{3,2,1,0:T(8,128)(2,1)} %param.11) | copy-start | bytes 6291460
  21.8 121.3 %all-gather.2.cloned.1.call-start = ((), (), s32[]{:S(2)}) async-start(), calls=%async_computation.3 | async-start | bytes 6291456 | tf_op jit(solution)/shard_map/all_gather | solution.py:58
  79.1 2.8 copy-start.4
  79.1 2.9 copy-start.5
  86.3 226.1 %reduce-scatter.4.cloned.1.call-start = ((), (), s32[]{:S(2)}) async-start(), calls=%async_computation.4 | async-start | bytes 10485760 | tf_op jit(solution)/shard_map/reduce_scatter | solution.py:90
  151.4 169.8 %reduce-scatter.6.cloned.1.call-start = ((), (), s32[]{:S(2)}) async-start(), calls=%async_computation.5 | async-start | bytes 10485760 | tf_op jit(solution)/shard_map/reduce_scatter | solution.py:93
  160.1 2.2 copy-start.6
  162.3 49.1 %collective-permute-start = (bf16[128,8192]{1,0:T(8,128)(2,1)S(1)}, bf16[128,8192]{1,0:T(8,128)(2,1)S(1)}, u32[]{:S(2)}, u32[]{:S(2)}) collective-permute-start(bf16[128,8192]{1,0:T(8,128)(2,1)S(1)} %copy-done.6), channel_id=1, source_target_pairs={{2,0},{4,2},{6,4},{3,1},{5,3},{7,5},{10,8},{12,10},{14,12},{11,9},... | collective-permute-start | bytes 6291464 | tf_op jit(solution)/shard_map/ppermute | solution.py:15
  211.3 51.2 %copy-start.2 = (f32[128,8192]{1,0:T(8,128)S(1)}, f32[128,8192]{1,0:T(8,128)}, u32[]{:S(2)}) copy-start(f32[128,8192]{1,0:T(8,128)} %get-tuple-element.8) | copy-start | bytes 12582916
  214.2 48.4 %collective-permute-start.1 = (bf16[128,8192]{1,0:T(8,128)(2,1)S(1)}, bf16[128,8192]{1,0:T(8,128)(2,1)S(1)}, u32[]{:S(2)}, u32[]{:S(2)}) collective-permute-start(bf16[128,8192]{1,0:T(8,128)(2,1)S(1)} %add_convert_fusion.2), channel_id=1, source_target_pairs={{2,0},{4,2},{6,4},{3,1},{5,3},{7,5},{10,8},{12,10},{14,12},{11,9},... | collective-permute-start | bytes 6291464 | tf_op jit(solution)/shard_map/ppermute | solution.py:15
  263.0 47.6 %collective-permute-start.2 = (bf16[128,8192]{1,0:T(8,128)(2,1)S(1)}, bf16[128,8192]{1,0:T(8,128)(2,1)S(1)}, u32[]{:S(2)}, u32[]{:S(2)}) collective-permute-start(bf16[128,8192]{1,0:T(8,128)(2,1)S(1)} %add_convert_fusion.1), channel_id=1, source_target_pairs={{2,0},{4,2},{6,4},{3,1},{5,3},{7,5},{10,8},{12,10},{14,12},{11,9},... | collective-permute-start | bytes 6291464 | tf_op jit(solution)/shard_map/ppermute | solution.py:15
  321.2 8.8 %copy-start.1 = (bf16[1,1,256,512]{3,2,1,0:T(8,128)(2,1)S(1)}, bf16[1,1,256,512]{3,2,1,0:T(8,128)(2,1)}, u32[]{:S(2)}) copy-start(bf16[1,1,256,512]{3,2,1,0:T(8,128)(2,1)} %param.14) | copy-start | bytes 786436
Sparse Core Ops, SparseCore 0:
  21.9 57.0 reduce-scatter.7
  86.4 56.7 all-gather.1
  151.5 71.3 reduce-scatter.3
  225.3 71.3 reduce-scatter.5
where the time goes:
time: 337 us; the launch traced here: 336 us
  waiting for transfers between devices  254 us (75%)
  matrix products  30.5 us (9%)
  other arithmetic  29.8 us (9%)
  between operations  13.9 us (4%)
  starting transfers between devices  4.21 us (1%)
  local copies, waits for them, and re-layouts  3.77 us (1%)
    ppermute x3, waiting for transfers between devices, from_behind(): return lax.ppermute(block, axis, route)  141 us
    all_gather x1, waiting for transfers between devices, local(): piece = lax.all_gather(normed, 'tensor', axis=0, tiled=True)  56.8 us
    reduce_scatter x1, waiting for transfers between devices, local(): lax.psum_scatter(((contract_cols(key_piece, weight_key) + contract_cols(v...  56.5 us
    dot_general x2, matrix products, contract_rows(): lax.dot_general(left, right, (((0,), (0,)), ((), ())), preferred_element_...  16.9 us
    dot_general x2, matrix products, contract_cols(): lax.dot_general(left, right, (((1,), (1,)), ((), ())), preferred_element_...  13.7 us
    broadcast_in_dim x1, other arithmetic, local(): momentum_value_new[None]  8.78 us
    broadcast_in_dim x1, other arithmetic, local(): momentum_key_new[None]  8.75 us
    convert_element_type x3, other arithmetic, local(): running.astype(jnp.bfloat16)  7.59 us
  transfers between devices with their start and end apart: 7, of which 5 were waited for; matrix products, arithmetic and copies ran while one was open for 7% of the time, Pallas kernels for 0%

commit v1 on v0

--- a/solution.py
+++ b/solution.py
@@ -2,6 +2,7 @@
 import jax.numpy as jnp
 from jax import lax
 from jax.sharding import PartitionSpec as P
+from jax.lax import axis_index, axis_size, ppermute
 
 epsilon = 1e-05
 inner_rate = 0.5
@@ -55,7 +56,16 @@
     value_rows = value_cot[0, 0]
     weight_key = local_key[0, 0]
     weight_value = local_value[0, 0]
-    piece = lax.all_gather(normed, "tensor", axis=0, tiled=True)
+    p_next = axis_size("tensor")
+    block_out = axis_index("tensor")
+    earlier, passed = (p_next, block_out)
+    piece, q_next = (normed, 1)
+    while q_next < earlier:
+        v1 = ppermute(piece, axis_name="tensor", perm=[(j0, j0 ^ q_next) for j0 in range(earlier)])
+        e_now = jnp.concatenate([piece, v1], axis=0)
+        parts_out = jnp.concatenate([v1, piece], axis=0)
+        piece = jnp.where(passed & q_next == 0, e_now, parts_out)
+        q_next = 2 * q_next
     key_piece = key_rows
     value_piece = value_rows
     grad_key = contract_rows(piece, key_piece)

time: 337 us -> 323 us (0.958)
  waiting for transfers between devices: 254 us -> 240 us
    all_gather x1 -> x0, waiting for transfers between devices: 56.8 us -> none  [local(): piece = lax.all_gather(normed, 'tensor', axis=0, tiled=True)]
    ppermute x0 -> x1, waiting for transfers between devices: none -> 47.1 us  [local(): ppermute(piece, axis_name='tensor', perm=[(j0, j0 ^ q_next) for j0 in ran...]
    ppermute x3, waiting for transfers between devices: 141 us -> 137 us  [from_behind(): return lax.ppermute(block, axis, route)]
where the time goes in v1:
time: 323 us
  waiting for transfers between devices  240 us (74%)
  matrix products  30.7 us (10%)
  other arithmetic  29.8 us (9%)
  between operations  13.8 us (4%)
  starting transfers between devices  4.53 us (1%)
  local copies, waits for them, and re-layouts  3.75 us (1%)
    ppermute x3, waiting for transfers between devices, from_behind(): return lax.ppermute(block, axis, route)  137 us
    reduce_scatter x1, waiting for transfers between devices, local(): lax.psum_scatter(((contract_cols(key_piece, weight_key) + contract_cols(v...  56.5 us
    ppermute x1, waiting for transfers between devices, local(): ppermute(piece, axis_name='tensor', perm=[(j0, j0 ^ q_next) for j0 in ran...  47.1 us
    dot_general x2, matrix products, contract_rows(): lax.dot_general(left, right, (((0,), (0,)), ((), ())), preferred_element_...  17 us
    dot_general x2, matrix products, contract_cols(): lax.dot_general(left, right, (((1,), (1,)), ((), ())), preferred_element_...  13.7 us
    broadcast_in_dim x1, other arithmetic, local(): momentum_value_new[None]  8.78 us
    broadcast_in_dim x1, other arithmetic, local(): momentum_key_new[None]  8.75 us
    convert_element_type x3, other arithmetic, local(): running.astype(jnp.bfloat16)  7.59 us
  transfers between devices with their start and end apart: 7, of which 5 were waited for; matrix products, arithmetic and copies ran while one was open for 7% of the time, Pallas kernels for 0%

profile of v1, /device:TPU:0, one launch (start us, length us, event | category | flops | bytes accessed | tf_op | source)
XLA Modules:
  0.0 322.9 jit_solution(1766624857557282295)
XLA Ops:
  7.2 0.0 copy-start
  7.2 0.0 copy-start.7
  7.2 0.0 reduce-scatter.8.cloned.1.call-start
  7.2 0.9 copy-done
  8.1 5.8 %fusion.3 = f32[256,8192]{1,0:T(8,128)S(1)} fusion(bf16[1,1,8192,512]{3,2,1,0:T(8,128)(2,1)} %param.16, bf16[1,1,256,512]{3,2,1,0:T(8,128)(2,1)S(1)} %copy-done), kind=kOutput, calls=%fused_computation.6 | convolution fusion | flops 2147483648 | bytes 17039360 | tf_op jit(solution)/shard_map/dot_general | solution.py:26
  13.9 7.9 %fusion.1 = bf16[256,8192]{1,0:T(8,128)(2,1)} fusion(f32[256,8192]{1,0:T(8,128)S(1)} %fusion.3, bf16[1,1,8192,512]{3,2,1,0:T(8,128)(2,1)} %param.17, bf16[1,1,256,512]{3,2,1,0:T(8,128)(2,1)S(1)} %copy-done.7), kind=kOutput, calls=%fused_computation.4 | convolution fusion | flops 2153775104 | bytes 21233664 | tf_op jit(solution)/shard_map/dot_general | solution.py:26
  21.8 0.0 reduce-scatter.8.cloned.1.call-update
  21.8 0.0 reduce-scatter.4.cloned.1.call-start
  21.9 0.7 copy-done.8
  22.6 56.5 %reduce-scatter.8.cloned.1.call-done = bf16[128,8192]{1,0:T(8,128)(2,1)} async-done(((bf16[256,8192]{1,0:T(8,128)(2,1)}), bf16[128,8192]{1,0:T(8,128)(2,1)}) %reduce-scatter.8.cloned.1.call-update) | async-done | bytes 2097168 | tf_op jit(solution)/shard_map/reduce_scatter | solution.py:77
  79.1 2.8 fusion.11
  81.9 0.0 copy-done.5
  81.9 4.3 %fusion.23 = (bf16[128,8192]{1,0:T(8,128)(2,1)}, f32[128,8192]{1,0:T(8,128)}, bf16[128,8192]{1,0:T(8,128)(2,1)}) fusion(bf16[1,128,8192]{2,1,0:T(8,128)(2,1)S(1)} %copy-done.5, f32[]{:T(128)S(6)} %convert_element_type.74, f32[128]{0:T(128)S(1)} %get-tuple-element.16, f32[128]{0:T(128)S(1)} %get-tuple-element.14, bf16[1,1,128,8192]{3,2,1,0:T(8,128)(2,1)S(1)} %copy-done.3, ...), kind=kLoop, calls=%fused_computation.44 | loop fusion | flops 14680064 | bytes 14714372 | tf_op jit(solution)/shard_map/convert_element_type | solution.py:94
  86.2 0.4 collective-permute-start
  86.6 47.1 %collective-permute-done = bf16[128,8192]{1,0:T(8,128)(2,1)S(1)} collective-permute-done((bf16[128,8192]{1,0:T(8,128)(2,1)}, bf16[128,8192]{1,0:T(8,128)(2,1)S(1)}, u32[]{:S(2)}, u32[]{:S(2)}) %collective-permute-start) | collective-permute-done | bytes 2097184 | tf_op jit(solution)/shard_map/ppermute | solution.py:64
  133.7 8.3 %subtract_convert_fusion.1 = bf16[8192,512]{1,0:T(8,128)(2,1)} fusion(bf16[1,1,8192,512]{3,2,1,0:T(8,128)(2,1)} %param.16, bf16[128,8192]{1,0:T(8,128)(2,1)S(1)} %collective-permute-done, bf16[128,8192]{1,0:T(8,128)(2,1)} %get-tuple-element.13, pred[]{:T(512)S(6)} %eq.6, bf16[1,1,256,512]{3,2,1,0:T(8,128)(2,1)S(1)} %copy-done), kind=kOutput, calls=%fused_computation.1 | convolution fusion | flops 2183135232 | bytes 21233664 | tf_op jit(solution)/shard_map/dot_general | solution.py:20
  142.0 0.0 reduce-scatter.4.cloned.1.call-update
  142.0 0.0 reduce-scatter.6.cloned.1.call-start
  142.1 8.7 %subtract_convert_fusion = bf16[8192,512]{1,0:T(8,128)(2,1)} fusion(bf16[1,1,8192,512]{3,2,1,0:T(8,128)(2,1)} %param.17, bf16[128,8192]{1,0:T(8,128)(2,1)S(1)} %collective-permute-done, bf16[128,8192]{1,0:T(8,128)(2,1)} %get-tuple-element.13, pred[]{:T(512)S(6)} %eq.6, bf16[1,1,256,512]{3,2,1,0:T(8,128)(2,1)S(1)} %copy-done.7), kind=kOutput, calls=%fused_computation | convolution fusion | flops 2183135232 | bytes 21233664 | tf_op jit(solution)/shard_map/dot_general | solution.py:20
  150.8 0.0 reduce-scatter.6.cloned.1.call-update
  150.8 2.1 copy-done.6
  152.9 1.3 collective-permute-start.1
  154.2 46.4 %collective-permute-done.1 = bf16[128,8192]{1,0:T(8,128)(2,1)S(1)} collective-permute-done((bf16[128,8192]{1,0:T(8,128)(2,1)S(1)}, bf16[128,8192]{1,0:T(8,128)(2,1)S(1)}, u32[]{:S(2)}, u32[]{:S(2)}) %collective-permute-start.1) | collective-permute-done | bytes 2097184 | tf_op jit(solution)/shard_map/ppermute | solution.py:16
  200.6 2.9 add_convert_fusion.2
  203.5 1.3 collective-permute-start.2
  204.8 45.6 %collective-permute-done.2 = bf16[128,8192]{1,0:T(8,128)(2,1)S(1)} collective-permute-done((bf16[128,8192]{1,0:T(8,128)(2,1)S(1)}, bf16[128,8192]{1,0:T(8,128)(2,1)S(1)}, u32[]{:S(2)}, u32[]{:S(2)}) %collective-permute-start.2) | collective-permute-done | bytes 2097184 | tf_op jit(solution)/shard_map/ppermute | solution.py:16
  250.5 0.4 add_convert_fusion.1
  250.9 1.5 collective-permute-start.3
  252.3 44.7 %collective-permute-done.3 = bf16[128,8192]{1,0:T(8,128)(2,1)S(1)} collective-permute-done((bf16[128,8192]{1,0:T(8,128)(2,1)S(1)}, bf16[128,8192]{1,0:T(8,128)(2,1)S(1)}, u32[]{:S(2)}, u32[]{:S(2)}) %collective-permute-start.3) | collective-permute-done | bytes 2097184 | tf_op jit(solution)/shard_map/ppermute | solution.py:16
  297.0 1.8 fusion.16
  298.8 8.7 %fusion.14 = (f32[1,2048,512]{2,1,0:T(8,128)}, f32[1,2048,512]{2,1,0:T(8,128)}) fusion(bf16[2048,512]{1,0:T(8,128)(2,1)} %reduce-scatter.4.cloned.1.call-done, f32[1,2048,512]{2,1,0:T(8,128)} %param.18, f32[1,2048,512]{2,1,0:T(8,128)} %param.20), kind=kLoop, calls=%fused_computation.32 | loop fusion | flops 9437184 | bytes 18874368 | tf_op jit(solution)/shard_map/broadcast_in_dim | solution.py:116
  307.6 8.8 %fusion.15 = (f32[1,2048,512]{2,1,0:T(8,128)}, f32[1,2048,512]{2,1,0:T(8,128)}) fusion(bf16[2048,512]{1,0:T(8,128)(2,1)} %reduce-scatter.6.cloned.1.call-done, f32[1,2048,512]{2,1,0:T(8,128)} %param.19, f32[1,2048,512]{2,1,0:T(8,128)} %param.21), kind=kLoop, calls=%fused_computation.33 | loop fusion | flops 9437184 | bytes 18874368 | tf_op jit(solution)/shard_map/broadcast_in_dim | solution.py:117
  (16 shorter events, 0.1 us)
Async XLA Ops:
  7.2 1.0 copy-start
  7.2 6.7 %copy-start.7 = (bf16[1,1,256,512]{3,2,1,0:T(8,128)(2,1)S(1)}, bf16[1,1,256,512]{3,2,1,0:T(8,128)(2,1)}, u32[]{:S(2)}) copy-start(bf16[1,1,256,512]{3,2,1,0:T(8,128)(2,1)} %param.15) | copy-start | bytes 786436
  7.2 71.9 %reduce-scatter.8.cloned.1.call-start = ((), (), s32[]{:S(2)}) async-start(), calls=%async_computation.5 | async-start | bytes 6291456 | tf_op jit(solution)/shard_map/reduce_scatter | solution.py:77
  21.8 0.8 copy-start.8
  21.8 57.3 %copy-start.3 = (bf16[1,1,128,8192]{3,2,1,0:T(8,128)(2,1)S(1)}, bf16[1,1,128,8192]{3,2,1,0:T(8,128)(2,1)}, u32[]{:S(2)}) copy-start(bf16[1,1,128,8192]{3,2,1,0:T(8,128)(2,1)} %param.11) | copy-start | bytes 6291460
  21.8 277.0 %reduce-scatter.4.cloned.1.call-start = ((), (), s32[]{:S(2)}) async-start(), calls=%async_computation.3 | async-start | bytes 10485760 | tf_op jit(solution)/shard_map/reduce_scatter | solution.py:100
  79.1 2.8 copy-start.4
  79.1 2.9 copy-start.5
  86.2 47.4 %collective-permute-start = (bf16[128,8192]{1,0:T(8,128)(2,1)}, bf16[128,8192]{1,0:T(8,128)(2,1)S(1)}, u32[]{:S(2)}, u32[]{:S(2)}) collective-permute-start(bf16[128,8192]{1,0:T(8,128)(2,1)} %get-tuple-element.13), channel_id=1, source_target_pairs={{0,1},{1,0},{2,3},{3,2},{4,5},{5,4},{6,7},{7,6},{8,9},{9,8},{10,11... | collective-permute-start | bytes 6291464 | tf_op jit(solution)/shard_map/ppermute | solution.py:64
  142.0 165.5 %reduce-scatter.6.cloned.1.call-start = ((), (), s32[]{:S(2)}) async-start(), calls=%async_computation.4 | async-start | bytes 10485760 | tf_op jit(solution)/shard_map/reduce_scatter | solution.py:103
  150.8 2.2 copy-start.6
  152.9 47.7 %collective-permute-start.1 = (bf16[128,8192]{1,0:T(8,128)(2,1)S(1)}, bf16[128,8192]{1,0:T(8,128)(2,1)S(1)}, u32[]{:S(2)}, u32[]{:S(2)}) collective-permute-start(bf16[128,8192]{1,0:T(8,128)(2,1)S(1)} %copy-done.6), channel_id=1, source_target_pairs={{2,0},{4,2},{6,4},{3,1},{5,3},{7,5},{10,8},{12,10},{14,12},{11,9},... | collective-permute-start | bytes 6291464 | tf_op jit(solution)/shard_map/ppermute | solution.py:16
  200.6 49.8 %copy-start.2 = (f32[128,8192]{1,0:T(8,128)S(1)}, f32[128,8192]{1,0:T(8,128)}, u32[]{:S(2)}) copy-start(f32[128,8192]{1,0:T(8,128)} %get-tuple-element.8) | copy-start | bytes 12582916
  203.5 46.9 %collective-permute-start.2 = (bf16[128,8192]{1,0:T(8,128)(2,1)S(1)}, bf16[128,8192]{1,0:T(8,128)(2,1)S(1)}, u32[]{:S(2)}, u32[]{:S(2)}) collective-permute-start(bf16[128,8192]{1,0:T(8,128)(2,1)S(1)} %add_convert_fusion.2), channel_id=1, source_target_pairs={{2,0},{4,2},{6,4},{3,1},{5,3},{7,5},{10,8},{12,10},{14,12},{11,9},... | collective-permute-start | bytes 6291464 | tf_op jit(solution)/shard_map/ppermute | solution.py:16
  250.9 46.2 %collective-permute-start.3 = (bf16[128,8192]{1,0:T(8,128)(2,1)S(1)}, bf16[128,8192]{1,0:T(8,128)(2,1)S(1)}, u32[]{:S(2)}, u32[]{:S(2)}) collective-permute-start(bf16[128,8192]{1,0:T(8,128)(2,1)S(1)} %add_convert_fusion.1), channel_id=1, source_target_pairs={{2,0},{4,2},{6,4},{3,1},{5,3},{7,5},{10,8},{12,10},{14,12},{11,9},... | collective-permute-start | bytes 6291464 | tf_op jit(solution)/shard_map/ppermute | solution.py:16
  307.6 8.8 %copy-start.1 = (bf16[1,1,256,512]{3,2,1,0:T(8,128)(2,1)S(1)}, bf16[1,1,256,512]{3,2,1,0:T(8,128)(2,1)}, u32[]{:S(2)}) copy-start(bf16[1,1,256,512]{3,2,1,0:T(8,128)(2,1)} %param.14) | copy-start | bytes 786436
Sparse Core Ops, SparseCore 0:
  21.9 57.0 reduce-scatter.7
  142.2 71.3 reduce-scatter.3
  216.2 71.3 reduce-scatter.5
